TPU v7x, 32 devices: a whole 2x2x4 slice. The times are simulated.
32 devices in a mesh: rep: 8 (over z, y), shard: 4 (over x, core).
Axes of the slice: x: 2, y: 2, z: 4, core: 2. Of those that a mesh axis runs over, the one named last changes fastest.
Arguments:
- hidden_in: bfloat16 [32768, 1024], P(('rep', 'shard')), may hold values from -6 to 6
- teacher: bfloat16 [32768, 1024], P(('rep', 'shard')), may hold values from -6 to 6
- cotangent: bfloat16 [32768, 1024], P(('rep', 'shard')), may hold values from -6 to 6
- lengths: int32 [32], P(('rep', 'shard')), may hold values from 512 to 1024, as said below
- norm_attn: float32 [1024], replicated, may hold values from 0.5 to 1.5
- w_in: bfloat16 [1024, 6144], P('shard'), may hold values from -0.1875 to 0.1875
- w_small: bfloat16 [1024, 24], P('shard'), may hold values from -0.1875 to 0.1875
- conv_w: float32 [4, 5120], replicated, may hold values from -3 to 3
- a_log: float32 [8], replicated, may hold values from -6 to 0.5
- dt_bias: float32 [8], replicated, may hold values from -2 to 1
- norm_head: float32 [128], replicated, may hold values from 0.5 to 1.5
- w_out: bfloat16 [1024, 1024], P('shard'), may hold values from -0.1875 to 0.1875
- norm_mlp: float32 [1024], replicated, may hold values from 0.5 to 1.5
- w_mlp_in: bfloat16 [1024, 5632], P('shard'), may hold values from -0.1875 to 0.1875
- w_mlp_down: bfloat16 [2816, 1024], P('shard'), may hold values from -0.109375 to 0.109375
Outputs:
- layer_out: bfloat16 [32768, 1024], P(('rep', 'shard'))
- loss: float32 [], replicated
- grad_hidden: bfloat16 [32768, 1024], P(('rep', 'shard'))
- grad_norm_attn: float32 [1024], replicated
- grad_w_in: float32 [1024, 6144], P('shard')
- grad_w_small: float32 [1024, 24], P('shard')
- grad_conv_w: float32 [4, 5120], replicated
- grad_a_log: float32 [8], replicated
- grad_dt_bias: float32 [8], replicated
- grad_norm_head: float32 [128], replicated
- grad_w_out: float32 [1024, 1024], P('shard')
- grad_norm_mlp: float32 [1024], replicated
- grad_w_mlp_in: float32 [1024, 5632], P('shard')
- grad_w_mlp_down: float32 [2816, 1024], P('shard')
Inputs may be any that keep to these rules, and one draw needn't show every extreme that they name: `lengths`: each sequence's valid slots are a prefix of its 1024 slots; in every draw some sequence is full and some holds 512 valid slots.
All inputs are finite; a program needn't handle non-finite values.
Results may differ from a plain program's by a relative error of at most 0.014.
Values may be sent and summed in bfloat16 or wider, within the bound.
No kernel may reach another device: no remote copies, remote signals or barrier semaphores. Data moves between devices by JAX's collectives and lax.ppermute only.
A program may use at most 512 MiB of HBM per device.

v0:
```python
import jax
import jax.numpy as jnp
from jax import lax
from jax.sharding import PartitionSpec as P

HEADS = 8
DK = 128
DV = 128
HOUSE = 2
BLOCK = 64
EPSILON = 1e-06
PRECISE = lax.Precision.HIGHEST


def norm_rows(row_values, gain_row):
    return (
        row_values
        * lax.rsqrt(jnp.mean(row_values * row_values, axis=-1, keepdims=True) + EPSILON)
        * gain_row
    )


def dot_plain(operand_a, operand_b):
    return jnp.dot(operand_a, operand_b, preferred_element_type=jnp.float32)


def dot_right_t(operand_a, operand_b):
    return lax.dot_general(
        operand_a, operand_b, (((1,), (1,)), ((), ())), preferred_element_type=jnp.float32
    )


def dot_left_t(operand_a, operand_b):
    return lax.dot_general(
        operand_a, operand_b, (((0,), (0,)), ((), ())), preferred_element_type=jnp.float32
    )


def block_coupling(keys_in, beta_rows, log_gates):
    row_count = keys_in.shape[0]
    cumulated = jnp.cumsum(log_gates, axis=0).T
    keys_head = jnp.transpose(keys_in, (1, 0, 2))
    betas_head = beta_rows.T
    row_index = lax.broadcasted_iota(jnp.int32, (row_count, row_count), 0)
    col_index = lax.broadcasted_iota(jnp.int32, (row_count, row_count), 1)
    strictly = (col_index < row_index)[None]
    spread_log = cumulated[:, :, None] - cumulated[:, None, :]
    fading = jnp.where(strictly, jnp.exp(jnp.where(strictly, spread_log, 0.0)), 0.0)
    intersections = jnp.einsum("hrc,hic->hri", keys_head, keys_head, precision=PRECISE)
    return intersections * fading * betas_head[:, None, :]


def block_step(memory, pieces):
    queries, keys_in, values_in, beta_rows, log_gates, inverse = pieces
    row_count = keys_in.shape[0]
    query_count = queries.shape[0]
    substeps = row_count // query_count
    cumulated = jnp.cumsum(log_gates, axis=0).T
    keys_head = jnp.transpose(keys_in, (1, 0, 2))
    values_head = jnp.transpose(values_in, (1, 0, 2))
    queries_head = jnp.transpose(queries, (1, 0, 2))
    betas_head = beta_rows.T
    carried = jnp.einsum("hrc,hcd->hrd", keys_head, memory, precision=PRECISE)
    targets = values_head - jnp.exp(cumulated)[:, :, None] * carried
    updates = jnp.einsum("hri,hid->hrd", inverse, targets, precision=PRECISE)
    read_row = (
        lax.broadcasted_iota(jnp.int32, (query_count, row_count), 0) * substeps + substeps - 1
    )
    read_col = lax.broadcasted_iota(jnp.int32, (query_count, row_count), 1)
    visible = (read_col <= read_row)[None]
    read_log = cumulated[:, substeps - 1 :: substeps]
    query_spread = read_log[:, :, None] - cumulated[:, None, :]
    query_fading = jnp.where(visible, jnp.exp(jnp.where(visible, query_spread, 0.0)), 0.0)
    scores = (
        jnp.einsum("htc,hic->hti", queries_head, keys_head, precision=PRECISE)
        * query_fading
        * betas_head[:, None, :]
    )
    outputs = jnp.exp(read_log)[:, :, None] * jnp.einsum(
        "htc,hcd->htd", queries_head, memory, precision=PRECISE
    )
    outputs = outputs + jnp.einsum("hti,hid->htd", scores, updates, precision=PRECISE)
    last_log = cumulated[:, -1]
    carry_weights = jnp.exp(last_log[:, None] - cumulated) * betas_head
    new_memory = jnp.exp(last_log)[:, None, None] * memory + jnp.einsum(
        "hic,hid->hcd", keys_head * carry_weights[:, :, None], updates, precision=PRECISE
    )
    return (new_memory, jnp.transpose(outputs, (1, 0, 2)))


def sequence_mix(queries, keys_in, values_in, beta_rows, log_gates):
    block_count = queries.shape[0] // BLOCK
    memory = jnp.zeros((HEADS, DK, DV), jnp.float32)
    keys_blocks = keys_in.reshape(block_count, BLOCK * HOUSE, HEADS, DK)
    beta_blocks = beta_rows.reshape(block_count, BLOCK * HOUSE, HEADS)
    gate_blocks = log_gates.reshape(block_count, BLOCK * HOUSE, HEADS)
    coupling = jax.vmap(block_coupling)(keys_blocks, beta_blocks, gate_blocks)
    identity = jnp.broadcast_to(jnp.eye(BLOCK * HOUSE, dtype=jnp.float32), coupling.shape)
    inverse = lax.linalg.triangular_solve(
        coupling, identity, left_side=True, lower=True, unit_diagonal=True
    )
    pieces = (
        queries.reshape(block_count, BLOCK, HEADS, DK),
        keys_blocks,
        values_in.reshape(block_count, BLOCK * HOUSE, HEADS, DV),
        beta_blocks,
        gate_blocks,
        inverse,
    )
    final_memory, outputs = lax.scan(jax.checkpoint(block_step), memory, pieces)
    return outputs.reshape(queries.shape[0], HEADS, DV)


def mixer_core(proj_rows, small_rows, conv_w, a_log, dt_bias, norm_head):
    slot_count = proj_rows.shape[0]
    tap_count = conv_w.shape[0]
    channel_count = conv_w.shape[1]
    conv_input = proj_rows[:, :channel_count]
    padded = jnp.concatenate(
        [jnp.zeros((tap_count - 1, channel_count), jnp.float32), conv_input], axis=0
    )
    conv_out = conv_w[0] * padded[0:slot_count]
    for offset in range(1, tap_count):
        conv_out = conv_out + conv_w[offset] * padded[offset : offset + slot_count]
    active = jax.nn.silu(conv_out)
    query_width = HEADS * DK
    key_width = HOUSE * HEADS * DK
    queries = active[:, :query_width].reshape(slot_count, HEADS, DK)
    keys_in = active[:, query_width : query_width + key_width].reshape(
        slot_count * HOUSE, HEADS, DK
    )
    values_in = active[:, query_width + key_width :].reshape(slot_count * HOUSE, HEADS, DV)
    queries = (
        queries
        * lax.rsqrt(jnp.sum(queries * queries, axis=-1, keepdims=True) + EPSILON)
        * DK ** (-0.5)
    )
    keys_in = keys_in * lax.rsqrt(jnp.sum(keys_in * keys_in, axis=-1, keepdims=True) + EPSILON)
    beta_rows = jax.nn.sigmoid(small_rows[:, : HOUSE * HEADS]).reshape(slot_count * HOUSE, HEADS)
    decays = -jnp.exp(a_log) * jax.nn.softplus(small_rows[:, HOUSE * HEADS :] + dt_bias)
    log_gates = jnp.concatenate(
        [decays[:, None, :], jnp.zeros((slot_count, HOUSE - 1, HEADS), jnp.float32)], axis=1
    ).reshape(slot_count * HOUSE, HEADS)
    mixed_heads = sequence_mix(queries, keys_in, values_in, beta_rows, log_gates)
    mixed_heads = (
        mixed_heads
        * lax.rsqrt(jnp.mean(mixed_heads * mixed_heads, axis=-1, keepdims=True) + EPSILON)
        * norm_head
    )
    out_gate = proj_rows[:, channel_count:].reshape(slot_count, HEADS, DV)
    return (mixed_heads * jax.nn.silu(out_gate)).reshape(slot_count, HEADS * DV)


def shards(
    hidden_in,
    teacher,
    cotangent,
    lengths,
    norm_attn,
    w_in,
    w_small,
    conv_w,
    a_log,
    dt_bias,
    norm_head,
    w_out,
    norm_mlp,
    w_mlp_in,
    w_mlp_down,
):
    row_count = hidden_in.shape[0]
    seq_here = lengths.shape[0]
    slot_count = row_count // seq_here
    own_rows = w_small.shape[0]
    w_in_all, w_small_all, w_out_all = (
        lax.all_gather(w_in, "shard", axis=0, tiled=True),
        lax.all_gather(w_small, "shard", axis=0, tiled=True),
        lax.all_gather(w_out, "shard", axis=0, tiled=True),
    )
    hidden32 = hidden_in.astype(jnp.float32)
    normed_in, norm_in_pull = jax.vjp(norm_rows, hidden32, norm_attn)
    normed_low = normed_in.astype(jnp.bfloat16)
    proj_rows = dot_plain(normed_low, w_in_all)
    small_rows = dot_plain(normed_low, w_small_all)

    def mixer_all(proj_part, small_part, conv_part, log_part, bias_part, gain_part):
        per_seq = jax.vmap(mixer_core, in_axes=(0, 0, None, None, None, None))(
            proj_part.reshape(seq_here, slot_count, proj_part.shape[1]),
            small_part.reshape(seq_here, slot_count, small_part.shape[1]),
            conv_part,
            log_part,
            bias_part,
            gain_part,
        )
        return per_seq.reshape(row_count, per_seq.shape[2])

    mixed_rows, mixer_pull = jax.vjp(
        mixer_all, proj_rows, small_rows, conv_w, a_log, dt_bias, norm_head
    )
    mixed_low = mixed_rows.astype(jnp.bfloat16)
    residual = hidden32 + dot_plain(mixed_low, w_out_all)
    w_mlp_in_all, w_down_all = (
        lax.all_gather(w_mlp_in, "shard", axis=0, tiled=True),
        lax.all_gather(w_mlp_down, "shard", axis=0, tiled=True),
    )
    normed_mid, norm_mid_pull = jax.vjp(norm_rows, residual, norm_mlp)
    mid_low = normed_mid.astype(jnp.bfloat16)
    gate_up = dot_plain(mid_low, w_mlp_in_all)
    unit_count = w_down_all.shape[0]
    gate_part = gate_up[:, :unit_count]
    up_part = gate_up[:, unit_count:]
    sigmoid_gate = jax.nn.sigmoid(gate_part)
    silu_gate = gate_part * sigmoid_gate
    product_low = (silu_gate * up_part).astype(jnp.bfloat16)
    output32 = residual + dot_plain(product_low, w_down_all)
    slot_index = lax.broadcasted_iota(jnp.int32, (seq_here, slot_count), 1)
    valid_rows = (slot_index < lengths[:, None]).astype(jnp.float32).reshape(row_count, 1)
    deviation = output32 - teacher.astype(jnp.float32)
    loss_sum, valid_count = lax.psum(
        (jnp.sum(valid_rows * deviation * deviation), jnp.sum(lengths).astype(jnp.float32)),
        ("rep", "shard"),
    )
    loss_value = loss_sum / (valid_count * output32.shape[1])
    grad_out = valid_rows * (cotangent.astype(jnp.float32) + deviation)
    grad_out_low = grad_out.astype(jnp.bfloat16)
    w_mlp_in_back, w_down_back = (
        lax.all_gather(w_mlp_in, "shard", axis=0, tiled=True),
        lax.all_gather(w_mlp_down, "shard", axis=0, tiled=True),
    )
    grad_product = dot_right_t(grad_out_low, w_down_back)
    grad_w_down = dot_left_t(product_low, grad_out_low)
    grad_gate = grad_product * up_part * sigmoid_gate * (1.0 + gate_part * (1.0 - sigmoid_gate))
    grad_up = grad_product * silu_gate
    grad_gate_up = jnp.concatenate([grad_gate, grad_up], axis=1).astype(jnp.bfloat16)
    grad_mid = dot_right_t(grad_gate_up, w_mlp_in_back)
    grad_w_mlp_in = dot_left_t(mid_low, grad_gate_up)
    grad_res_part, grad_norm_mlp = norm_mid_pull(grad_mid)
    grad_residual = grad_out + grad_res_part
    own_mlp_in, own_down = (
        lax.psum_scatter(
            grad_w_mlp_in.astype(jnp.bfloat16), "shard", scatter_dimension=0, tiled=True
        ).astype(jnp.float32),
        lax.psum_scatter(
            grad_w_down.astype(jnp.bfloat16), "shard", scatter_dimension=0, tiled=True
        ).astype(jnp.float32),
    )
    grad_res_low = grad_residual.astype(jnp.bfloat16)
    w_in_back, w_small_back, w_out_back = (
        lax.all_gather(w_in, "shard", axis=0, tiled=True),
        lax.all_gather(w_small, "shard", axis=0, tiled=True),
        lax.all_gather(w_out, "shard", axis=0, tiled=True),
    )
    grad_mixed = dot_right_t(grad_res_low, w_out_back)
    grad_w_out = dot_left_t(mixed_low, grad_res_low)
    grad_proj, grad_small, grad_conv, grad_log, grad_bias, grad_gain = mixer_pull(grad_mixed)
    grad_proj_low = grad_proj.astype(jnp.bfloat16)
    grad_small_low = grad_small.astype(jnp.bfloat16)
    grad_normed = dot_right_t(grad_proj_low, w_in_back) + dot_right_t(grad_small_low, w_small_back)
    grad_w_in = dot_left_t(normed_low, grad_proj_low)
    grad_w_small = dot_left_t(normed_low, grad_small_low)
    grad_in_part, grad_norm_attn = norm_in_pull(grad_normed)
    grad_hidden = (grad_residual + grad_in_part).astype(jnp.bfloat16)
    sum_norm_attn, sum_conv, sum_log, sum_bias, sum_gain, sum_norm_mlp, sum_small = lax.psum(
        (grad_norm_attn, grad_conv, grad_log, grad_bias, grad_gain, grad_norm_mlp, grad_w_small),
        ("rep", "shard"),
    )
    own_small = lax.dynamic_slice_in_dim(sum_small, lax.axis_index("shard") * own_rows, own_rows, 0)
    own_in, own_out = (
        lax.psum_scatter(
            grad_w_in.astype(jnp.bfloat16), "shard", scatter_dimension=0, tiled=True
        ).astype(jnp.float32),
        lax.psum_scatter(
            grad_w_out.astype(jnp.bfloat16), "shard", scatter_dimension=0, tiled=True
        ).astype(jnp.float32),
    )
    own_in, own_out, own_mlp_in, own_down = (
        lax.psum(own_in.astype(jnp.bfloat16), "rep").astype(jnp.float32),
        lax.psum(own_out.astype(jnp.bfloat16), "rep").astype(jnp.float32),
        lax.psum(own_mlp_in.astype(jnp.bfloat16), "rep").astype(jnp.float32),
        lax.psum(own_down.astype(jnp.bfloat16), "rep").astype(jnp.float32),
    )
    return (
        output32.astype(jnp.bfloat16),
        loss_value,
        grad_hidden,
        sum_norm_attn,
        own_in,
        own_small,
        sum_conv,
        sum_log,
        sum_bias,
        sum_gain,
        own_out,
        sum_norm_mlp,
        own_mlp_in,
        own_down,
    )


def solution(mesh):
    in_specs = (
        P(("rep", "shard"), None),
        P(("rep", "shard"), None),
        P(("rep", "shard"), None),
        P(("rep", "shard")),
        P(),
        P("shard", None),
        P("shard", None),
        P(),
        P(),
        P(),
        P(),
        P("shard", None),
        P(),
        P("shard", None),
        P("shard", None),
    )
    out_specs = (
        P(("rep", "shard"), None),
        P(),
        P(("rep", "shard"), None),
        P(),
        P("shard", None),
        P("shard", None),
        P(),
        P(),
        P(),
        P(),
        P("shard", None),
        P(),
        P("shard", None),
        P("shard", None),
    )
    return jax.shard_map(shards, mesh=mesh, in_specs=in_specs, out_specs=out_specs, check_vma=False)
```

profile of v0, /device:TPU:0, one launch (start us, length us, event | category | flops | bytes accessed | tf_op | source)
XLA Modules:
  0.0 4014.8 jit_solution(10543486210761847069)
XLA Ops:
  42.4 52.0 %all-gather.5.cloned.1.call-done = bf16[1024,6144]{1,0:T(8,128)(2,1)} async-done(((bf16[256,6144]{1,0:T(8,128)(2,1)}), bf16[1024,6144]{1,0:T(8,128)(2,1)}) %all-gather.5.cloned.1.call-update) | async-done | bytes 12582928 | tf_op jit(solution)/shard_map/all_gather | solution.py:176
  94.4 21.1 convolution_bitcast_fusion.8
  115.5 16.8 slice.113
  132.4 45.0 %fusion.127 = (f32[1,1024,5120]{2,1,0:T(8,128)}, f32[1,1024,5120]{2,1,0:T(8,128)}) fusion(f32[1,1024,5120]{2,1,0:T(8,128)} %slice.113, f32[5120]{0:T(1024)S(1)} %bitcast.855, f32[5120]{0:T(1024)S(1)} %bitcast.857, f32[5120]{0:T(1024)S(1)} %bitcast.853, f32[5120]{0:T(1024)S(1)} %bitcast.851), kind=kLoop, calls=%fused_computation.197 | loop fusion | flops 57671680 | bytes 62996480 | tf_op jit(solution)/shard_map/jvp(vmap(jit(silu)))/mul | solution.py:125
  177.4 11.0 fusion.234
  238.9 21.6 fusion.134
  268.9 1259.0 %custom-call.5 = f32[1,16,8,1,128,128]{4,5,3,2,1,0:T(8,128)} custom-call(f32[1,16,8,1,128,128]{5,4,3,2,1,0:T(8,128)} %add_bitcast_fusion), custom_call_target="InvertDiagBlocksLowerTriangular" | custom-call | tf_op jit(solution)/shard_map/jvp(vmap())/triangular_solve | solution.py:99
  1550.8 16.6 fusion.140
  1571.7 316.9 %while.47 = (s32[]{:T(128)}, f32[1,8,128,128]{3,2,1,0:T(8,128)S(1)}, f32[16,1,64,8,128]{4,2,3,1,0:T(8,128)}, f32[16,1,8,128,128]{4,3,2,1,0:T(8,128)}, f32[16,1,1...) while((s32[]{:T(128)}, ...), condition=%wide.region_6.7_spmd.clone.clone, body=%wide.region_4.6_spmd.clone.clone.sunk | while | flops 907740160 | bytes 11392390 | solution.py:110
  1913.3 21.1 fusion.224
  1934.4 12.2 multiply_convert_fusion.2
  1946.6 13.7 fusion.190
  1960.3 20.2 multiply_convert_fusion.1
  1980.5 21.4 multiply_reduce_fusion.9
  2002.0 10.3 fusion.153
  2074.6 1061.4 %while.46 = (s32[]{:T(128)}, f32[1,8,128,128]{2,3,1,0:T(8,128)}, f32[16,1,64,8,128]{4,3,2,0,1:T(8,128)}, f32[16,1,128,8,128]{4,2,3,0,1:T(8,128)}, f32[16,1,128,8...) while((s32[]{:T(128)}, f32[1,8,128,128]{2,3,1,0:T(8,128)}, ...), condition=%wide.region_25.26_spmd.clone, body=%wide.region_14.25_spmd.clone.sunk | while | flops 2421509120 | bytes 52434800 | solution.py:110
  3142.2 21.0 fusion.136
  3163.1 19.9 convolution_convert_fusion.1
  3209.7 22.6 fusion.226
  3232.4 16.9 fusion.130
  3249.3 22.4 bitcast_add_fusion.4
  3348.6 13.1 add_add_fusion
  3361.8 44.9 %multiply_reduce_fusion.4 = (f32[5120]{0:T(1024)S(1)}, f32[5120]{0:T(1024)S(1)}, f32[5120]{0:T(1024)S(1)}, f32[5120]{0:T(1024)S(1)}, f32[1,1024,5120]{2,1,0:T(8,128)}) fusion(f32[1,1024,5120]{2,1,0:T(8,128)} %slice.113, f32[1,1024,6144]{2,1,0:T(8,128)} %convolution_bitcast_fusion.8, f32[1,1024,5120]{2,1,0:T(8,128)} %get-tuple-element.897, ...), kind=kLoop, calls=%fused_computation.194 | loop fusion | flops 99594240 | bytes 104939520 | tf_op jit(solution)/shard_map/transpose(jvp(vmap()))/reduce_sum | solution.py:124
  3406.7 34.0 broadcast_multiply_fusion
  3440.7 36.1 pad_add_fusion
  3476.9 19.9 convolution_convert_fusion
  3503.4 23.3 fusion.236
  3531.6 65.4 %reduce-scatter.5.cloned.1.call-done = bf16[256,6144]{1,0:T(8,128)(2,1)} async-done(((bf16[1024,6144]{1,0:T(8,128)(2,1)}), bf16[256,6144]{1,0:T(8,128)(2,1)}) %reduce-scatter.5.cloned.1.call-update) | async-done | bytes 3145744 | tf_op jit(solution)/shard_map/reduce_scatter | solution.py:269
  3599.9 22.3 fusion.151
  3622.2 40.0 all-reduce.19
  3677.2 49.2 %all-reduce.25.cloned.1.call-done = (f32[1024,24]{0,1:T(8,128)}, f32[4,5120]{1,0:T(4,128)}) async-done(((f32[1024,24]{0,1:T(8,128)}, f32[4,5120]{1,0:T(4,128)}), (f32[1024,24]{0,1:T(8,128)}, f32[4,5120]{1,0:T(4,128)})) %all-reduce.25.cloned.1.call-update) | async-done | bytes 180240 | tf_op jit(solution)/shard_map/psum | solution.py:263
  3727.8 266.4 %all-reduce.27.cloned.1.call-done = (bf16[256,6144]{1,0:T(8,128)(2,1)}, bf16[256,1024]{1,0:T(8,128)(2,1)}, bf16[256,5632]{1,0:T(8,128)(2,1)}, bf16[704,1024]{1,0:T(8,128)(2,1)}) async-done(((bf16[256,6144]{1,0:T(8,128)(2,1)}, bf16[256,1024]{1,0:T(8,128)(2,1)}, bf16[256,5632]{1,0:T(8,128)(2,1)}, bf16[704,1024]{1,0:T(8,128)(2,1)}), (bf16[256,6144]{1,0:T(8,128)(2,1)}, bf16[256,1024]{1,0:T(8,128)(2,1)}, ...) | async-done | bytes 7995408 | tf_op jit(solution)/shard_map/psum | solution.py:277
  (2118 shorter events, 1730.6 us)
Async XLA Ops:
  7.2 87.2 %all-gather.5.cloned.1.call-start = ((), (), s32[]{:S(2)}) async-start(), calls=%async_computation.4 | async-start | bytes 15728640 | tf_op jit(solution)/shard_map/all_gather | solution.py:176
  7.9 1898.5 %all-gather.7.cloned.1.call-start = ((), (), s32[]{:S(2)}) async-start(), calls=%async_computation.5 | async-start | bytes 2621440 | tf_op jit(solution)/shard_map/all_gather | solution.py:178
  8.7 1904.6 %all-gather.9.cloned.1.call-start = ((), (), s32[]{:S(2)}) async-start(), calls=%async_computation.6 | async-start | bytes 14417920 | tf_op jit(solution)/shard_map/all_gather | solution.py:203
  9.4 1937.2 %all-gather.11.cloned.1.call-start = ((), (), s32[]{:S(2)}) async-start(), calls=%async_computation.7 | async-start | bytes 7208960 | tf_op jit(solution)/shard_map/all_gather | solution.py:204
  10.0 3521.6 %reduce-scatter.7.cloned.1.call-start = ((), (), s32[]{:S(2)}) async-start(), calls=%async_computation.9 | async-start | bytes 2621440 | tf_op jit(solution)/shard_map/reduce_scatter | solution.py:272
  12.9 1893.5 %copy-start.17 = (bf16[1024,1024]{0,1:T(8,128)(2,1)}, bf16[1024,1024]{0,1:T(8,128)(2,1)S(1)}, u32[]{:S(2)}) copy-start(bf16[1024,1024]{0,1:T(8,128)(2,1)S(1)} %copy.300) | copy-start | bytes 6291460
  13.5 80.9 %copy-start.74 = (f32[1024]{0:T(1024)}, f32[1024]{0:T(1024)S(1)}, u32[]{:S(2)}) copy-start(f32[1024]{0:T(1024)S(1)} %fusion.214) | copy-start | bytes 12292
  26.2 106.2 %copy-start.59 = (f32[1,5120]{1,0:T(1,128)}, f32[1,5120]{1,0:T(1,128)S(1)}, u32[]{:S(2)}) copy-start(f32[1,5120]{1,0:T(1,128)S(1)} %get-tuple-element.929) | copy-start | bytes 61444
  26.2 106.2 %copy-start.61 = (f32[1,5120]{1,0:T(1,128)}, f32[1,5120]{1,0:T(1,128)S(1)}, u32[]{:S(2)}) copy-start(f32[1,5120]{1,0:T(1,128)S(1)} %get-tuple-element.930) | copy-start | bytes 61444
  26.2 106.2 %copy-start.63 = (f32[1,5120]{1,0:T(1,128)}, f32[1,5120]{1,0:T(1,128)S(1)}, u32[]{:S(2)}) copy-start(f32[1,5120]{1,0:T(1,128)S(1)} %get-tuple-element.931) | copy-start | bytes 61444
  27.9 232.6 %copy-start.37 = (f32[16,8,128]{2,1,0:T(8,128)}, f32[16,8,128]{2,1,0:T(8,128)S(1)}, u32[]{:S(2)}) copy-start(f32[16,8,128]{2,1,0:T(8,128)S(1)} %copy.311) | copy-start | bytes 196612
  32.4 228.1 %copy-start.26 = (f32[16,8,128]{2,1,0:T(8,128)}, f32[16,8,128]{2,1,0:T(8,128)S(1)}, u32[]{:S(2)}) copy-start(f32[16,8,128]{2,1,0:T(8,128)S(1)} %copy.308) | copy-start | bytes 196612
  32.5 228.0 %copy-start.53 = (pred[128,128]{1,0:T(8,128)(4,1)}, pred[128,128]{1,0:T(8,128)(4,1)S(1)}, u32[]{:S(2)}) copy-start(pred[128,128]{1,0:T(8,128)(4,1)S(1)} %get-tuple-element.944) | copy-start | bytes 49156
  32.5 228.0 %copy-start.55 = (pred[128,128]{1,0:T(8,128)(4,1)}, pred[128,128]{1,0:T(8,128)(4,1)S(1)}, u32[]{:S(2)}) copy-start(pred[128,128]{1,0:T(8,128)(4,1)S(1)} %get-tuple-element.945) | copy-start | bytes 49156
  1913.3 88.7 %copy-start.77 = (f32[1024]{0:T(1024)}, f32[1024]{0:T(1024)S(1)}, u32[]{:S(2)}) copy-start(f32[1024]{0:T(1024)S(1)} %fusion.215) | copy-start | bytes 12292
  2035.4 1496.2 %reduce-scatter.11.cloned.1.call-start = ((), (), s32[]{:S(2)}) async-start(), calls=%async_computation.11 | async-start | bytes 7208960 | tf_op jit(solution)/shard_map/reduce_scatter | solution.py:243
  2057.5 1474.1 %reduce-scatter.9.cloned.1.call-start = ((), (), s32[]{:S(2)}) async-start(), calls=%async_computation.10 | async-start | bytes 14417920 | tf_op jit(solution)/shard_map/reduce_scatter | solution.py:240
  3183.1 413.9 %reduce-scatter.5.cloned.1.call-start = ((), (), s32[]{:S(2)}) async-start(), calls=%async_computation.8 | async-start | bytes 15728640 | tf_op jit(solution)/shard_map/reduce_scatter | solution.py:269
  3209.7 39.6 slice-start.2
  3361.8 44.9 %copy-start.60 = (f32[1,5120]{1,0:T(1,128)S(1)}, f32[1,5120]{1,0:T(1,128)}, u32[]{:S(2)}) copy-start(f32[1,5120]{1,0:T(1,128)} %copy-done.59) | copy-start | bytes 61444
  3361.8 44.9 %copy-start.62 = (f32[1,5120]{1,0:T(1,128)S(1)}, f32[1,5120]{1,0:T(1,128)}, u32[]{:S(2)}) copy-start(f32[1,5120]{1,0:T(1,128)} %copy-done.61) | copy-start | bytes 61444
  3361.8 44.9 %copy-start.64 = (f32[1,5120]{1,0:T(1,128)S(1)}, f32[1,5120]{1,0:T(1,128)}, u32[]{:S(2)}) copy-start(f32[1,5120]{1,0:T(1,128)} %copy-done.63) | copy-start | bytes 61444
  3361.8 44.9 %copy-start.66 = (f32[1,5120]{1,0:T(1,128)S(1)}, f32[1,5120]{1,0:T(1,128)}, u32[]{:S(2)}) copy-start(f32[1,5120]{1,0:T(1,128)} %get-tuple-element.932) | copy-start | bytes 61444
  3440.7 36.2 copy-start.18
  3440.7 36.2 copy-start.75
  3440.7 36.2 copy-start.84
  3496.8 229.7 %all-reduce.25.cloned.1.call-start = ((), (), s32[]{:S(2)}) async-start(), calls=%async_computation.12 | async-start | bytes 360448 | tf_op jit(solution)/shard_map/psum | solution.py:263
  3497.7 30.0 copy-start.48
  3528.7 68.4 %copy-start.94 = (f32[8]{0:T(128)S(1)}, f32[8]{0:T(128)}, u32[]{:S(2)}) copy-start(f32[8]{0:T(128)} %param.27) | copy-start | bytes 100
  3528.7 68.4 %copy-start.58 = (bf16[1024,24]{0,1:T(8,128)(2,1)S(1)}, bf16[1024,24]{0,1:T(8,128)(2,1)}, u32[]{:S(2)}) copy-start(bf16[1024,24]{0,1:T(8,128)(2,1)} %copy-done.57) | copy-start | bytes 147460
  3531.5 462.8 %all-reduce.27.cloned.1.call-start = ((), (), s32[]{:S(2)}) async-start(), calls=%async_computation.13 | async-start | bytes 15990784 | tf_op jit(solution)/shard_map/psum | solution.py:277
  3599.9 66.3 %copy-start.73 = (f32[1024]{0:T(1024)S(1)}, f32[1024]{0:T(1024)}, u32[]{:S(2)}) copy-start(f32[1024]{0:T(1024)} %copy-done.72) | copy-start | bytes 12292
  (305 other events, 2538.5 us)
Sparse Core Ops, SparseCore 0:
  9.6 84.7 all-gather.4
  96.0 22.5 all-gather.6
  120.2 76.1 all-gather.8
  197.8 43.3 all-gather.10
  2035.6 31.9 reduce-scatter.6
  2070.7 54.8 reduce-scatter.10
  3183.2 92.8 reduce-scatter.8
  3496.9 100.0 reduce-scatter.4
  3603.8 122.6 all-reduce.24
  3730.8 263.4 all-reduce.26
where the time goes:
time: 4050 us; the launch traced here: 4010 us
  other arithmetic  1700 us (42%)
  matrix products  992 us (24%)
  local copies, waits for them, and re-layouts  812 us (20%)
  waiting for transfers between devices  436 us (11%)
  blocking collectives  46.2 us (1%)
    another operation x4, other arithmetic, sequence_mix(): lax.linalg.triangular_solve(coupling, identity, left_side=True, lower=Tru...  1260 us
    psum x1, waiting for transfers between devices, shards(): lax.psum(own_in.astype(jnp.bfloat16), 'rep').astype(jnp.float32)  266 us
    dot_general x64, matrix products, block_step(): updates = jnp.einsum('hri,hid->hrd', inverse, targets, precision=PRECISE)  145 us
    dynamic_update_slice x128, local copies, waits for them, and re-layouts, sequence_mix(): final_memory, outputs = lax.scan(jax.checkpoint(block_step), memory, pieces)  144 us
    dot_general x64, matrix products, block_step(): jnp.einsum('htc,hic->hti', queries_head, keys_head, precision=PRECISE)  129 us
    dot_general x64, matrix products, block_step(): jnp.einsum('htc,hcd->htd', queries_head, memory, precision=PRECISE)  123 us
    dot_general x48, matrix products, block_step(): jnp.einsum('hic,hid->hcd', keys_head * carry_weights[:, :, None], updates...  119 us
    dot_general x64, matrix products, block_step(): carried = jnp.einsum('hrc,hcd->hrd', keys_head, memory, precision=PRECISE)  86.5 us
  transfers between devices with their start and end apart: 10, of which 4 were waited for; matrix products, arithmetic and copies ran while one was open for 84% of the time, Pallas kernels for 0%

commit v1 on v0

--- a/solution.py
+++ b/solution.py
@@ -274,7 +274,7 @@
         ).astype(jnp.float32),
     )
     own_in, own_out, own_mlp_in, own_down = (
-        lax.psum(own_in.astype(jnp.bfloat16), "rep").astype(jnp.float32),
+        jnp.sum(lax.all_gather(own_in.astype(jnp.bfloat16), "rep"), axis=0).astype(jnp.float32),
         lax.psum(own_out.astype(jnp.bfloat16), "rep").astype(jnp.float32),
         lax.psum(own_mlp_in.astype(jnp.bfloat16), "rep").astype(jnp.float32),
         lax.psum(own_down.astype(jnp.bfloat16), "rep").astype(jnp.float32),

time: 4050 us -> 4270 us (1.054)
  waiting for transfers between devices: 436 us -> 821 us
  local copies, waits for them, and re-layouts: 812 us -> 708 us
  matrix products: 992 us -> 914 us
    all_gather x0 -> x1, waiting for transfers between devices: none -> 473 us  [shards(): lax.all_gather(own_in.astype(jnp.bfloat16), 'rep')]
    psum x1, waiting for transfers between devices: 266 us -> 178 us  [shards(): lax.psum(own_out.astype(jnp.bfloat16), 'rep').astype(jnp.float32)]
    dot_general x64, matrix products: 123 us -> 71.5 us  [block_step(): jnp.einsum('htc,hcd->htd', queries_head, memory, precision=PRECISE)]
    dynamic_update_slice x128, local copies, waits for them, and re-layouts: 144 us -> 98.6 us  [sequence_mix(): final_memory, outputs = lax.scan(jax.checkpoint(block_step), memory, pieces)]
  transfers between devices with their start and end apart: 10 -> 11, of which waited for: 4 -> 5; matrix products, arithmetic and copies ran while one was open for 84% -> 76% of each run, Pallas kernels for 0% -> 0%
where the time goes in v1:
time: 4270 us; the launch traced here: 4240 us
  other arithmetic  1730 us (41%)
  matrix products  914 us (21%)
  waiting for transfers between devices  821 us (19%)
  local copies, waits for them, and re-layouts  708 us (17%)
  blocking collectives  46.3 us (1%)
    another operation x4, other arithmetic, sequence_mix(): lax.linalg.triangular_solve(coupling, identity, left_side=True, lower=Tru...  1260 us
    all_gather x1, waiting for transfers between devices, shards(): lax.all_gather(own_in.astype(jnp.bfloat16), 'rep')  473 us
    psum x1, waiting for transfers between devices, shards(): lax.psum(own_out.astype(jnp.bfloat16), 'rep').astype(jnp.float32)  178 us
    dot_general x64, matrix products, block_step(): updates = jnp.einsum('hri,hid->hrd', inverse, targets, precision=PRECISE)  148 us
    dot_general x64, matrix products, block_step(): jnp.einsum('htc,hic->hti', queries_head, keys_head, precision=PRECISE)  133 us
    dynamic_update_slice x128, local copies, waits for them, and re-layouts, sequence_mix(): final_memory, outputs = lax.scan(jax.checkpoint(block_step), memory, pieces)  98.6 us
    dot_general x48, matrix products, block_step(): jnp.einsum('hti,hid->htd', scores, updates, precision=PRECISE)  88.1 us
    dot_general x48, matrix products, block_step(): jnp.einsum('hic,hid->hcd', keys_head * carry_weights[:, :, None], updates...  86.5 us
  transfers between devices with their start and end apart: 11, of which 5 were waited for; matrix products, arithmetic and copies ran while one was open for 76% of the time, Pallas kernels for 0%

profile of v1, /device:TPU:0, one launch (start us, length us, event | category | flops | bytes accessed | tf_op | source)
XLA Modules:
  0.0 4243.8 jit_solution(540427983366676674)
XLA Ops:
  41.9 52.5 %all-gather.7.cloned.1.call-done = bf16[1024,6144]{1,0:T(8,128)(2,1)} async-done(((bf16[256,6144]{1,0:T(8,128)(2,1)}), bf16[1024,6144]{1,0:T(8,128)(2,1)}) %all-gather.7.cloned.1.call-update) | async-done | bytes 12582928 | tf_op jit(solution)/shard_map/all_gather | solution.py:176
  94.4 21.1 convolution_bitcast_fusion.8
  115.5 16.8 slice.113
  132.3 45.1 %fusion.127 = (f32[1,1024,5120]{2,1,0:T(8,128)}, f32[1,1024,5120]{2,1,0:T(8,128)}) fusion(f32[1,1024,5120]{2,1,0:T(8,128)} %slice.113, f32[5120]{0:T(1024)S(1)} %bitcast.852, f32[5120]{0:T(1024)S(1)} %bitcast.854, f32[5120]{0:T(1024)S(1)} %bitcast.850, f32[5120]{0:T(1024)S(1)} %bitcast.848), kind=kLoop, calls=%fused_computation.197 | loop fusion | flops 57671680 | bytes 62996480 | tf_op jit(solution)/shard_map/jvp(vmap(jit(silu)))/mul | solution.py:125
  229.7 24.9 fusion.134
  263.2 1258.9 %custom-call.5 = f32[1,16,8,1,128,128]{4,5,3,2,1,0:T(8,128)} custom-call(f32[1,16,8,1,128,128]{5,4,3,2,1,0:T(8,128)} %add_bitcast_fusion), custom_call_target="InvertDiagBlocksLowerTriangular" | custom-call | tf_op jit(solution)/shard_map/jvp(vmap())/triangular_solve | solution.py:99
  1551.6 16.7 fusion.140
  1572.7 279.7 %while.47 = (s32[]{:T(128)}, f32[1,8,128,128]{3,2,1,0:T(8,128)S(1)}, f32[16,1,64,8,128]{4,2,3,1,0:T(8,128)}, f32[16,1,8,128,128]{4,3,2,1,0:T(8,128)}, f32[16,1,1...) while((s32[]{:T(128)}, ...), condition=%wide.region_6.7_spmd.clone.clone, body=%wide.region_4.6_spmd.clone.clone.sunk | while | flops 907740160 | bytes 11395430 | solution.py:110
  1877.0 20.9 fusion.224
  1898.0 12.2 multiply_convert_fusion.2
  1910.2 13.7 fusion.190
  1923.8 20.3 multiply_convert_fusion.1
  1944.1 21.4 multiply_reduce_fusion.9
  2031.8 941.0 %while.46 = (s32[]{:T(128)}, f32[1,8,128,128]{2,3,1,0:T(8,128)S(1)}, f32[16,1,64,8,128]{4,3,2,0,1:T(8,128)}, f32[16,1,128,8,128]{4,2,3,0,1:T(8,128)}, f32[16,1,1...) while((s32[]{:T(128)}, ...), condition=%wide.region_25.26_spmd.clone, body=%wide.region_14.25_spmd.clone.sunk | while | flops 2421509120 | bytes 48215644 | solution.py:110
  2972.8 23.1 fusion.136
  2996.0 19.9 convolution_convert_fusion.1
  3016.8 22.4 fusion.226
  3039.2 16.5 fusion.130
  3055.7 22.6 bitcast_add_fusion.4
  3180.8 13.3 add_add_fusion
  3194.1 44.8 %multiply_reduce_fusion.4 = (f32[5120]{0:T(1024)S(1)}, f32[5120]{0:T(1024)S(1)}, f32[5120]{0:T(1024)S(1)}, f32[5120]{0:T(1024)S(1)}, f32[1,1024,5120]{2,1,0:T(8,128)}) fusion(f32[1,1024,5120]{2,1,0:T(8,128)} %slice.113, f32[1,1024,6144]{2,1,0:T(8,128)} %convolution_bitcast_fusion.8, f32[1,1024,5120]{2,1,0:T(8,128)} %get-tuple-element.896, ...), kind=kLoop, calls=%fused_computation.194 | loop fusion | flops 99594240 | bytes 104939520 | tf_op jit(solution)/shard_map/transpose(jvp(vmap()))/reduce_sum | solution.py:124
  3239.0 34.0 broadcast_multiply_fusion
  3273.0 36.1 pad_add_fusion
  3309.1 19.6 convolution_convert_fusion
  3330.1 23.3 fusion.236
  3362.7 64.6 %reduce-scatter.5.cloned.1.call-done = bf16[256,6144]{1,0:T(8,128)(2,1)} async-done(((bf16[1024,6144]{1,0:T(8,128)(2,1)}), bf16[256,6144]{1,0:T(8,128)(2,1)}) %reduce-scatter.5.cloned.1.call-update) | async-done | bytes 3145744 | tf_op jit(solution)/shard_map/reduce_scatter | solution.py:269
  3430.2 22.3 fusion.151
  3452.5 40.1 all-reduce.19
  3507.7 49.1 %all-reduce.25.cloned.1.call-done = (f32[1024,24]{0,1:T(8,128)}, f32[4,5120]{1,0:T(4,128)}) async-done(((f32[1024,24]{0,1:T(8,128)}, f32[4,5120]{1,0:T(4,128)}), (f32[1024,24]{0,1:T(8,128)}, f32[4,5120]{1,0:T(4,128)})) %all-reduce.25.cloned.1.call-update) | async-done | bytes 180240 | tf_op jit(solution)/shard_map/psum | solution.py:263
  3558.1 178.4 %all-reduce.27.cloned.1.call-done = (bf16[256,1024]{1,0:T(8,128)(2,1)}, bf16[256,5632]{1,0:T(8,128)(2,1)}, bf16[704,1024]{1,0:T(8,128)(2,1)}) async-done(((bf16[256,1024]{1,0:T(8,128)(2,1)}, bf16[256,5632]{1,0:T(8,128)(2,1)}, bf16[704,1024]{1,0:T(8,128)(2,1)}), (bf16[256,1024]{1,0:T(8,128)(2,1)}, bf16[256,5632]{1,0:T(8,128)(2,1)}, bf16[704,1024]{1,0:T(8,128)(2,1)})) %all-reduce.27.cloned.1.call-update) | async-done | bytes 4849680 | tf_op jit(solution)/shard_map/psum | solution.py:278
  3744.7 472.8 %all-gather.15.cloned.1.call-done = bf16[2048,6144]{1,0:T(8,128)(2,1)} async-done(((bf16[256,6144]{1,0:T(8,128)(2,1)}), bf16[2048,6144]{1,0:T(8,128)(2,1)}) %all-gather.15.cloned.1.call-update) | async-done | bytes 25165840 | tf_op jit(solution)/shard_map/all_gather | solution.py:277
  4217.5 14.0 reduce_sum.331
  (1955 shorter events, 1577.5 us)
Async XLA Ops:
  7.2 87.2 %all-gather.7.cloned.1.call-start = ((), (), s32[]{:S(2)}) async-start(), calls=%async_computation.4 | async-start | bytes 15728640 | tf_op jit(solution)/shard_map/all_gather | solution.py:176
  7.9 1862.2 %all-gather.9.cloned.1.call-start = ((), (), s32[]{:S(2)}) async-start(), calls=%async_computation.5 | async-start | bytes 2621440 | tf_op jit(solution)/shard_map/all_gather | solution.py:178
  8.7 1868.3 %all-gather.11.cloned.1.call-start = ((), (), s32[]{:S(2)}) async-start(), calls=%async_computation.6 | async-start | bytes 14417920 | tf_op jit(solution)/shard_map/all_gather | solution.py:203
  9.4 1900.7 %all-gather.13.cloned.1.call-start = ((), (), s32[]{:S(2)}) async-start(), calls=%async_computation.7 | async-start | bytes 7208960 | tf_op jit(solution)/shard_map/all_gather | solution.py:204
  10.0 3352.1 %reduce-scatter.7.cloned.1.call-start = ((), (), s32[]{:S(2)}) async-start(), calls=%async_computation.9 | async-start | bytes 2621440 | tf_op jit(solution)/shard_map/reduce_scatter | solution.py:272
  13.0 1857.2 %copy-start.13 = (bf16[1024,1024]{0,1:T(8,128)(2,1)}, bf16[1024,1024]{0,1:T(8,128)(2,1)S(1)}, u32[]{:S(2)}) copy-start(bf16[1024,1024]{0,1:T(8,128)(2,1)S(1)} %copy.300) | copy-start | bytes 6291460
  14.3 80.2 %copy-start.68 = (f32[1024]{0:T(1024)}, f32[1024]{0:T(1024)S(1)}, u32[]{:S(2)}) copy-start(f32[1024]{0:T(1024)S(1)} %fusion.214) | copy-start | bytes 12292
  24.4 107.8 %copy-start.53 = (f32[1,5120]{1,0:T(1,128)}, f32[1,5120]{1,0:T(1,128)S(1)}, u32[]{:S(2)}) copy-start(f32[1,5120]{1,0:T(1,128)S(1)} %get-tuple-element.928) | copy-start | bytes 61444
  24.4 107.8 %copy-start.55 = (f32[1,5120]{1,0:T(1,128)}, f32[1,5120]{1,0:T(1,128)S(1)}, u32[]{:S(2)}) copy-start(f32[1,5120]{1,0:T(1,128)S(1)} %get-tuple-element.929) | copy-start | bytes 61444
  24.5 107.8 %copy-start.57 = (f32[1,5120]{1,0:T(1,128)}, f32[1,5120]{1,0:T(1,128)S(1)}, u32[]{:S(2)}) copy-start(f32[1,5120]{1,0:T(1,128)S(1)} %get-tuple-element.930) | copy-start | bytes 61444
  24.5 107.8 %copy-start.59 = (f32[1,5120]{1,0:T(1,128)}, f32[1,5120]{1,0:T(1,128)S(1)}, u32[]{:S(2)}) copy-start(f32[1,5120]{1,0:T(1,128)S(1)} %get-tuple-element.931) | copy-start | bytes 61444
  31.0 223.7 %copy-start.22 = (f32[16,8,128]{2,1,0:T(8,128)}, f32[16,8,128]{2,1,0:T(8,128)S(1)}, u32[]{:S(2)}) copy-start(f32[16,8,128]{2,1,0:T(8,128)S(1)} %copy.308) | copy-start | bytes 196612
  32.5 222.2 %copy-start.34 = (f32[16,8,128]{2,1,0:T(8,128)}, f32[16,8,128]{2,1,0:T(8,128)S(1)}, u32[]{:S(2)}) copy-start(f32[16,8,128]{2,1,0:T(8,128)S(1)} %copy.311) | copy-start | bytes 196612
  32.6 222.1 %copy-start.47 = (pred[128,128]{1,0:T(8,128)(4,1)}, pred[128,128]{1,0:T(8,128)(4,1)S(1)}, u32[]{:S(2)}) copy-start(pred[128,128]{1,0:T(8,128)(4,1)S(1)} %get-tuple-element.943) | copy-start | bytes 49156
  32.6 222.1 %copy-start.49 = (pred[128,128]{1,0:T(8,128)(4,1)}, pred[128,128]{1,0:T(8,128)(4,1)S(1)}, u32[]{:S(2)}) copy-start(pred[128,128]{1,0:T(8,128)(4,1)S(1)} %get-tuple-element.944) | copy-start | bytes 49156
  229.7 1292.4 %copy-start.29 = (f32[16,128,8]{1,2,0:T(8,128)}, f32[16,128,8]{1,2,0:T(8,128)S(1)}, u32[]{:S(2)}) copy-start(f32[16,128,8]{1,2,0:T(8,128)S(1)} %get-tuple-element.933) | copy-start | bytes 196612
  1877.0 88.6 %copy-start.70 = (f32[1024]{0:T(1024)}, f32[1024]{0:T(1024)S(1)}, u32[]{:S(2)}) copy-start(f32[1024]{0:T(1024)S(1)} %fusion.215) | copy-start | bytes 12292
  1981.7 1380.5 %reduce-scatter.11.cloned.1.call-start = ((), (), s32[]{:S(2)}) async-start(), calls=%async_computation.11 | async-start | bytes 7208960 | tf_op jit(solution)/shard_map/reduce_scatter | solution.py:243
  2013.5 1348.7 %reduce-scatter.9.cloned.1.call-start = ((), (), s32[]{:S(2)}) async-start(), calls=%async_computation.10 | async-start | bytes 14417920 | tf_op jit(solution)/shard_map/reduce_scatter | solution.py:240
  3015.9 411.4 %reduce-scatter.5.cloned.1.call-start = ((), (), s32[]{:S(2)}) async-start(), calls=%async_computation.8 | async-start | bytes 15728640 | tf_op jit(solution)/shard_map/reduce_scatter | solution.py:269
  3016.8 39.0 slice-start
  3194.1 44.9 %copy-start.54 = (f32[1,5120]{1,0:T(1,128)S(1)}, f32[1,5120]{1,0:T(1,128)}, u32[]{:S(2)}) copy-start(f32[1,5120]{1,0:T(1,128)} %copy-done.53) | copy-start | bytes 61444
  3194.1 44.9 %copy-start.56 = (f32[1,5120]{1,0:T(1,128)S(1)}, f32[1,5120]{1,0:T(1,128)}, u32[]{:S(2)}) copy-start(f32[1,5120]{1,0:T(1,128)} %copy-done.55) | copy-start | bytes 61444
  3194.1 44.9 %copy-start.58 = (f32[1,5120]{1,0:T(1,128)S(1)}, f32[1,5120]{1,0:T(1,128)}, u32[]{:S(2)}) copy-start(f32[1,5120]{1,0:T(1,128)} %copy-done.57) | copy-start | bytes 61444
  3194.1 44.9 %copy-start.60 = (f32[1,5120]{1,0:T(1,128)S(1)}, f32[1,5120]{1,0:T(1,128)}, u32[]{:S(2)}) copy-start(f32[1,5120]{1,0:T(1,128)} %copy-done.59) | copy-start | bytes 61444
  3273.0 36.1 copy-start.77
  3328.7 228.0 %all-reduce.25.cloned.1.call-start = ((), (), s32[]{:S(2)}) async-start(), calls=%async_computation.13 | async-start | bytes 360448 | tf_op jit(solution)/shard_map/psum | solution.py:263
  3359.9 67.4 %copy-start.88 = (f32[8]{0:T(128)S(1)}, f32[8]{0:T(128)}, u32[]{:S(2)}) copy-start(f32[8]{0:T(128)} %param.27) | copy-start | bytes 100
  3360.0 67.4 %copy-start.52 = (bf16[1024,24]{0,1:T(8,128)(2,1)S(1)}, bf16[1024,24]{0,1:T(8,128)(2,1)}, u32[]{:S(2)}) copy-start(bf16[1024,24]{0,1:T(8,128)(2,1)} %copy-done.51) | copy-start | bytes 147460
  3362.1 374.4 %all-reduce.27.cloned.1.call-start = ((), (), s32[]{:S(2)}) async-start(), calls=%async_computation.14 | async-start | bytes 9699328 | tf_op jit(solution)/shard_map/psum | solution.py:278
  3362.7 854.8 %all-gather.15.cloned.1.call-start = ((), (), s32[]{:S(2)}) async-start(), calls=%async_computation.12 | async-start | bytes 28311552 | tf_op jit(solution)/shard_map/all_gather | solution.py:277
  3430.2 62.4 %copy-start.67 = (f32[1024]{0:T(1024)S(1)}, f32[1024]{0:T(1024)}, u32[]{:S(2)}) copy-start(f32[1024]{0:T(1024)} %copy-done.66) | copy-start | bytes 12292
  (223 other events, 1604.3 us)
Sparse Core Ops, SparseCore 0:
  9.6 84.7 all-gather.6
  96.0 22.6 all-gather.8
  120.2 76.1 all-gather.10
  197.8 43.3 all-gather.12
  1981.8 31.6 reduce-scatter.6
  2016.6 54.8 reduce-scatter.10
  3016.1 92.0 reduce-scatter.8
  3328.8 98.4 reduce-scatter.4
  3434.1 122.5 all-reduce.24
  3560.6 175.8 all-reduce.26
  3738.1 479.3 all-gather.14
